TPU v7x, 32 devices: a whole 2x2x4 slice. The times are simulated.
32 devices in a mesh: batch: 4 (over y, x), seq: 4 (over z), head: 2 (over core).
Axes of the slice: x: 2, y: 2, z: 4, core: 2. Of those that a mesh axis runs over, the one named last changes fastest.
Arguments:
- hidden: bfloat16 [4, 2048, 1024], P('batch', 'seq', 'head'), may hold values from -6 to 6
- norm_gain: bfloat16 [1024], P('head'), may hold values from 0.099609375 to 1.8984375
- gate_weight: bfloat16 [1024, 2048], P(None, 'head'), may hold values from -0.1875 to 0.1875
- inner_weight: bfloat16 [1024, 2048], P(None, 'head'), may hold values from -0.1875 to 0.1875
- step_weight: bfloat16 [1024, 32], P(None, 'head'), may hold values from -0.375 to 0.375
- maps_weight: bfloat16 [1024, 256], replicated, may hold values from -0.1875 to 0.1875
- inner_kernel: float32 [4, 2048], P(None, 'head'), may hold values from -3 to 3
- inner_bias: float32 [2048], P('head'), may hold values from -1 to 1
- maps_kernel: float32 [4, 256], replicated, may hold values from -3 to 3
- maps_bias: float32 [256], replicated, may hold values from -1 to 1
- step_bias: float32 [32], P('head'), may hold values from -7 to -5
- decay_log: float32 [32], P('head'), may hold values from -5.3 to 1
- skip_gain: float32 [32], P('head'), may hold values from 1 to 4
- gate_gain: float32 [2048], P('head'), may hold values from 0.1 to 1.9
- output_weight: bfloat16 [2048, 1024], P('head'), may hold values from -0.125 to 0.125
- cotangent: bfloat16 [4, 2048, 1024], P('batch', 'seq', 'head'), may hold values from -6 to 6
Outputs:
- output: float32 [4, 2048, 1024], P('batch', 'seq', 'head')
- grad_hidden: float32 [4, 2048, 1024], P('batch', 'seq', 'head')
- grad_norm_gain: float32 [1024], P('head')
- grad_gate_weight: float32 [1024, 2048], P(None, 'head')
- grad_inner_weight: float32 [1024, 2048], P(None, 'head')
- grad_step_weight: float32 [1024, 32], P(None, 'head')
- grad_maps_weight: float32 [1024, 256], replicated
- grad_inner_kernel: float32 [4, 2048], P(None, 'head')
- grad_inner_bias: float32 [2048], P('head')
- grad_maps_kernel: float32 [4, 256], replicated
- grad_maps_bias: float32 [256], replicated
- grad_step_bias: float32 [32], P('head')
- grad_decay_log: float32 [32], P('head')
- grad_skip_gain: float32 [32], P('head')
- grad_gate_gain: float32 [2048], P('head')
- grad_output_weight: float32 [2048, 1024], P('head')
All inputs are finite; a program needn't handle non-finite values.
Results may differ from a plain program's by a relative error of at most 0.0089.
Values may be sent and summed in bfloat16 or wider, within the bound.
A program may use at most 192 MiB of HBM per device.

v0:
```python
import jax
import jax.numpy as jnp
from jax import lax
from jax.sharding import PartitionSpec as P

D = 1024
HEADDIM = 64
STATE = 128
CONV = 4
GROUP = 256
DI = 2048
HIGH = lax.Precision.HIGHEST
EPSILON = 1e-05


def shifted(array, axis, by):
    count = lax.axis_size(axis)
    pairs = [(i, i + by) for i in range(count) if 0 <= i + by < count]
    return lax.ppermute(array, axis, pairs)


def entering(array, axis, combine, identity, reverse):
    count, index = (lax.axis_size(axis), lax.axis_index(axis))
    everything = jax.tree.map(lambda part: lax.all_gather(part, axis), array)
    start = jax.tree.map(
        lambda part, zero: jnp.broadcast_to(jnp.asarray(zero, part.dtype), part.shape),
        array,
        identity,
    )

    def step(k, before):
        at = count - 1 - k if reverse else k
        reached = at > index if reverse else at < index
        new = combine(before, jax.tree.map(lambda part: part[at], everything))
        return jax.tree.map(lambda a, b: jnp.where(reached, a, b), new, before)

    return lax.fori_loop(0, count, step, start)


def silu_slope(values):
    sigmoid = jax.nn.sigmoid(values)
    return sigmoid * (1.0 + values * (1.0 - sigmoid))


def ssd_blocks(inner_act, write_map, read_map, step_size, decay_rates, initial):
    length, heads, headdim = inner_act.shape
    blocks_count = length // GROUP
    inner_blocks = inner_act.reshape(blocks_count, GROUP, heads, headdim)
    write_blocks = write_map.reshape(blocks_count, GROUP, write_map.shape[-1])
    read_blocks = read_map.reshape(blocks_count, GROUP, read_map.shape[-1])
    step_blocks = step_size.reshape(blocks_count, GROUP, heads)
    causal = (jnp.arange(GROUP)[:, None] >= jnp.arange(GROUP)[None, :])[:, :, None]

    def advance(state_in, pieces):
        inner_part, write_part, read_part, step_part = pieces
        cumlog = jnp.cumsum(step_part * decay_rates[None, :], axis=0)
        spread = jnp.where(causal, cumlog[:, None, :] - cumlog[None, :, :], 0.0)
        decays = jnp.where(causal, jnp.exp(spread), 0.0)
        scores = jnp.dot(read_part, write_part.T, precision=HIGH)
        weighted = inner_part * step_part[:, :, None]
        within = jnp.einsum("tsh,shp->thp", decays * scores[:, :, None], weighted, precision=HIGH)
        carried = jnp.einsum("tn,hpn->thp", read_part, state_in, precision=HIGH)
        result = within + jnp.exp(cumlog)[:, :, None] * carried
        remain = jnp.exp(cumlog[-1][None, :] - cumlog)
        fresh = jnp.einsum("shp,sn->hpn", weighted * remain[:, :, None], write_part, precision=HIGH)
        state_out = jnp.exp(cumlog[-1])[:, None, None] * state_in + fresh
        return (state_out, result)

    final, outputs = lax.scan(
        advance, initial, (inner_blocks, write_blocks, read_blocks, step_blocks)
    )
    return (outputs.reshape(length, heads, headdim), final)


def batched_scan(inner_heads, write_map, read_map, step_size, decay_rates, state_in):
    return jax.vmap(ssd_blocks, in_axes=(0, 0, 0, 0, None, 0))(
        inner_heads, write_map, read_map, step_size, decay_rates, state_in
    )


def chain_pair(earlier, later):
    return (earlier[0] * later[0], earlier[1] * later[0][:, :, None, None] + later[1])


def conv_apply(padded, kernel, bias_row, length):
    summed = bias_row
    for offset in range(kernel.shape[0]):
        summed = summed + kernel[offset] * padded[..., offset : offset + length, :]
    return summed


def conv_grads(padded, extended, grad_out, kernel, length):
    leading = tuple(range(grad_out.ndim - 1))
    grad_kernel = jnp.stack(
        [
            jnp.sum(grad_out * padded[..., offset : offset + length, :], axis=leading)
            for offset in range(kernel.shape[0])
        ]
    )
    grad_bias = jnp.sum(grad_out, axis=leading)
    width_less = kernel.shape[0] - 1
    grad_input = jnp.zeros_like(grad_out)
    for offset in range(kernel.shape[0]):
        begin_at = width_less - offset
        grad_input = grad_input + kernel[offset] * extended[..., begin_at : begin_at + length, :]
    return (grad_input, grad_kernel, grad_bias)


def on_device(
    hidden,
    norm_gain,
    gate_weight,
    inner_weight,
    step_weight,
    maps_weight,
    inner_kernel,
    inner_bias,
    maps_kernel,
    maps_bias,
    step_bias,
    decay_log,
    skip_gain,
    gate_gain,
    output_weight,
    cotangent,
):
    seq_count, tok_count, local_width = hidden.shape
    rows_count = seq_count * tok_count
    local_inner = gate_weight.shape[1]
    heads_local = step_weight.shape[1]
    whole_hidden, whole_cotangent, whole_gain = (
        lax.all_gather(hidden, "head", axis=2, tiled=True),
        lax.all_gather(cotangent, "head", axis=2, tiled=True),
        lax.all_gather(norm_gain, "head", axis=0, tiled=True),
    )
    residual = whole_hidden.reshape(rows_count, D).astype(jnp.float32)
    inverse = lax.rsqrt(jnp.mean(residual * residual, axis=-1, keepdims=True) + EPSILON)
    normal = residual * inverse
    normed = (normal * whole_gain.astype(jnp.float32)).astype(jnp.bfloat16)
    gate_pre = jnp.dot(normed, gate_weight, preferred_element_type=jnp.float32)
    inner_pre = jnp.dot(normed, inner_weight, preferred_element_type=jnp.float32)
    maps_pre = jnp.dot(normed, maps_weight, preferred_element_type=jnp.float32)
    step_pre = jnp.dot(normed, step_weight, preferred_element_type=jnp.float32).reshape(
        seq_count, tok_count, heads_local
    )
    inner_seq = inner_pre.reshape(seq_count, tok_count, local_inner)
    maps_seq = maps_pre.reshape(seq_count, tok_count, 2 * STATE)
    edge_inner, edge_maps = shifted(
        (inner_seq[:, tok_count - (CONV - 1) :, :], maps_seq[:, tok_count - (CONV - 1) :, :]),
        "seq",
        1,
    )
    inner_pad = jnp.concatenate([edge_inner, inner_seq], axis=1)
    maps_pad = jnp.concatenate([edge_maps, maps_seq], axis=1)
    inner_conv = conv_apply(inner_pad, inner_kernel, inner_bias, tok_count)
    maps_conv = conv_apply(maps_pad, maps_kernel, maps_bias, tok_count)
    inner_act = jax.nn.silu(inner_conv)
    maps_act = jax.nn.silu(maps_conv)
    write_map = maps_act[..., :STATE]
    read_map = maps_act[..., STATE:]
    step_size = jax.nn.softplus(step_pre + step_bias)
    decay_rates = -jnp.exp(decay_log)
    inner_heads = inner_act.reshape(seq_count, tok_count, heads_local, HEADDIM)
    zero_state = jnp.zeros((seq_count, heads_local, HEADDIM, STATE), jnp.float32)
    local_mix, local_state = batched_scan(
        inner_heads, write_map, read_map, step_size, decay_rates, zero_state
    )
    cumlog = jnp.cumsum(step_size * decay_rates, axis=1)
    total_decay = jnp.exp(cumlog[:, -1, :])
    identity = (jnp.ones_like(total_decay), jnp.zeros_like(local_state))
    prefix_decay, state_in = entering(
        (total_decay, local_state), "seq", chain_pair, identity, False
    )
    carried = jnp.einsum("stn,shpn->sthp", read_map, state_in, precision=HIGH)
    mixed_out = (
        local_mix
        + jnp.exp(cumlog)[..., None] * carried
        + skip_gain[None, None, :, None] * inner_heads
    )
    mixed_flat = mixed_out.reshape(rows_count, local_inner)
    gate_act = jax.nn.silu(gate_pre)
    gated_val = mixed_flat * gate_act
    square_total = lax.psum(jnp.sum(gated_val * gated_val, axis=-1), "head")
    scale_back = lax.rsqrt(square_total[:, None] / DI + EPSILON)
    gated_norm = (gated_val * scale_back * gate_gain).astype(jnp.bfloat16)
    branch_part = jnp.dot(gated_norm, output_weight, preferred_element_type=jnp.float32)
    branch = lax.psum_scatter(branch_part, "head", scatter_dimension=1, tiled=True)
    output = (hidden.reshape(rows_count, local_width).astype(jnp.float32) + branch).reshape(
        seq_count, tok_count, local_width
    )
    cot_rows = whole_cotangent.reshape(rows_count, D)
    grad_output_weight = jnp.dot(gated_norm.T, cot_rows, preferred_element_type=jnp.float32)
    grad_norm_out = jnp.dot(cot_rows, output_weight.T, preferred_element_type=jnp.float32)
    grad_gate_gain = jnp.sum(grad_norm_out * gated_val * scale_back, axis=0)
    grad_scaled = grad_norm_out * gate_gain
    dot_total = lax.psum(jnp.sum(grad_scaled * gated_val, axis=-1), "head")
    grad_gated = scale_back * (
        grad_scaled - gated_val * scale_back * scale_back * (dot_total[:, None] / DI)
    )
    grad_mixed = (grad_gated * gate_act).reshape(seq_count, tok_count, heads_local, HEADDIM)
    grad_gate_pre = grad_gated * mixed_flat * silu_slope(gate_pre)
    grad_skip_gain = jnp.sum(grad_mixed * inner_heads, axis=(0, 1, 3))
    from_here = jnp.einsum(
        "sthp,stn->shpn", grad_mixed * jnp.exp(cumlog)[..., None], read_map, precision=HIGH
    )
    suffix_decay, state_grad = entering((total_decay, from_here), "seq", chain_pair, identity, True)
    recomputed, scan_back = jax.vjp(
        batched_scan, inner_heads, write_map, read_map, step_size, decay_rates, state_in
    )
    grad_inner_heads, grad_write, grad_read, grad_step, grad_rates, grad_start = scan_back(
        (grad_mixed, state_grad)
    )
    grad_write, grad_read = lax.psum((grad_write, grad_read), "head")
    grad_maps = jnp.concatenate([grad_write, grad_read], axis=-1)
    grad_inner = (grad_inner_heads + skip_gain[None, None, :, None] * grad_mixed).reshape(
        seq_count, tok_count, local_inner
    )
    grad_inner_conv = grad_inner * silu_slope(inner_conv)
    grad_maps_conv = grad_maps * silu_slope(maps_conv)
    next_inner, next_maps = shifted(
        (grad_inner_conv[:, : CONV - 1, :], grad_maps_conv[:, : CONV - 1, :]), "seq", -1
    )
    inner_ext = jnp.concatenate([grad_inner_conv, next_inner], axis=1)
    maps_ext = jnp.concatenate([grad_maps_conv, next_maps], axis=1)
    grad_inner_pre, grad_inner_kernel, grad_inner_bias = conv_grads(
        inner_pad, inner_ext, grad_inner_conv, inner_kernel, tok_count
    )
    grad_maps_pre, grad_maps_kernel, grad_maps_bias = conv_grads(
        maps_pad, maps_ext, grad_maps_conv, maps_kernel, tok_count
    )
    grad_step_pre = grad_step * jax.nn.sigmoid(step_pre + step_bias)
    grad_step_bias = jnp.sum(grad_step_pre, axis=(0, 1))
    grad_decay_log = grad_rates * decay_rates
    gate_round = grad_gate_pre.astype(jnp.bfloat16)
    inner_round = grad_inner_pre.reshape(rows_count, local_inner).astype(jnp.bfloat16)
    maps_round = grad_maps_pre.reshape(rows_count, 2 * STATE).astype(jnp.bfloat16)
    step_round = grad_step_pre.reshape(rows_count, heads_local).astype(jnp.bfloat16)
    grad_gate_weight = jnp.dot(normed.T, gate_round, preferred_element_type=jnp.float32)
    grad_inner_weight = jnp.dot(normed.T, inner_round, preferred_element_type=jnp.float32)
    grad_maps_weight = jnp.dot(normed.T, maps_round, preferred_element_type=jnp.float32)
    grad_step_weight = jnp.dot(normed.T, step_round, preferred_element_type=jnp.float32)
    partial_normed = jnp.dot(gate_round, gate_weight.T, preferred_element_type=jnp.float32)
    partial_normed = partial_normed + jnp.dot(
        inner_round, inner_weight.T, preferred_element_type=jnp.float32
    )
    partial_normed = partial_normed + jnp.dot(
        step_round, step_weight.T, preferred_element_type=jnp.float32
    )
    input_share = lax.psum_scatter(partial_normed, "head", scatter_dimension=1, tiled=True)
    column_start = lax.axis_index("head") * local_width
    maps_rows = lax.dynamic_slice_in_dim(maps_weight, column_start, local_width, 0)
    input_share = input_share + jnp.dot(maps_round, maps_rows.T, preferred_element_type=jnp.float32)
    normal_local = lax.dynamic_slice_in_dim(normal, column_start, local_width, 1)
    grad_normal = input_share * norm_gain.astype(jnp.float32)
    dot_sum = lax.psum(jnp.sum(grad_normal * normal_local, axis=-1), "head")
    grad_rows = inverse * (grad_normal - normal_local * (dot_sum[:, None] / D)) + cotangent.reshape(
        rows_count, local_width
    ).astype(jnp.float32)
    grad_hidden = grad_rows.reshape(seq_count, tok_count, local_width)
    grad_norm_gain = jnp.sum(input_share * normal_local, axis=0)
    summed = lax.psum(
        (
            grad_norm_gain,
            grad_gate_weight,
            grad_inner_weight,
            grad_step_weight,
            grad_maps_weight,
            grad_inner_kernel,
            grad_inner_bias,
            grad_maps_kernel,
            grad_maps_bias,
            grad_step_bias,
            grad_decay_log,
            grad_skip_gain,
            grad_gate_gain,
            grad_output_weight,
        ),
        ("batch", "seq"),
    )
    return (
        output,
        grad_hidden,
        summed[0],
        summed[1],
        summed[2],
        summed[3],
        summed[4],
        summed[5],
        summed[6],
        summed[7],
        summed[8],
        summed[9],
        summed[10],
        summed[11],
        summed[12],
        summed[13],
    )


def solution(mesh):
    return jax.shard_map(
        on_device,
        mesh=mesh,
        in_specs=(
            P("batch", "seq", "head"),
            P("head"),
            P(None, "head"),
            P(None, "head"),
            P(None, "head"),
            P(),
            P(None, "head"),
            P("head"),
            P(),
            P(),
            P("head"),
            P("head"),
            P("head"),
            P("head"),
            P("head", None),
            P("batch", "seq", "head"),
        ),
        out_specs=(
            P("batch", "seq", "head"),
            P("batch", "seq", "head"),
            P("head"),
            P(None, "head"),
            P(None, "head"),
            P(None, "head"),
            P(),
            P(None, "head"),
            P("head"),
            P(),
            P(),
            P("head"),
            P("head"),
            P("head"),
            P("head"),
            P("head", None),
        ),
        check_vma=False,
    )
```

profile of v0, /device:TPU:0, one launch (start us, length us, event | category | flops | bytes accessed | tf_op | source)
XLA Modules:
  0.0 855.7 jit_solution(2560668838805555344)
XLA Ops:
  13.6 7.7 all-gather.8.cloned.1.call-done
  24.9 3.8 collective-permute-start.1
  31.4 3.4 collective-permute-start
  43.4 3.5 reshape_reshape.7
  46.9 3.2 copy.229
  50.1 70.7 %while.120 = (s32[]{:T(128)}, f32[1,16,64,128]{3,2,1,0:T(8,128)}, f32[2,1,256,16,64]{2,0,4,3,1:T(2,128)}, f32[2,1,256,16]{2,0,3,1:T(2,128)}, f32[16]{0:T(128)S(1...) while((s32[]{:T(128)}, f32[1,16,64,128]{3,2,1,0:T(8,128)}, ...), condition=%wide.region_4.5_spmd.clone.clone, body=%wide.region_1.4_spmd.clone.clone.sunk | while | flops 1717903360 | bytes 23170916 | solution.py:69
  53.6 4.8 fusion.317
  59.5 21.9 %dynamic_update_slice.235 = f32[2,1,256,16,64]{2,0,4,3,1:T(2,128)} dynamic-update-slice(f32[2,1,256,16,64]{2,0,4,3,1:T(2,128)} %get-tuple-element.2732, f32[1,1,256,16,64]{2,0,4,3,1:T(1,128)S(1)} %copy.413, s32[]{:T(128)} %get-tuple-element.2730, s32[]{:T(128)} %constant.258.clone.1..sunk.3, s32[]{:T(128)} %constant.258.clone.1..sunk.3, s32[]{:T(128)} %constant.258.clone.1..sunk.3, ...) | dynamic-update-slice | bytes 2097156 | tf_op jit(solution)/shard_map/vmap()/while/body/jit(dynamic_update_index_in_dim)/dynamic_update_slice | solution.py:69
  81.8 3.0 fusion.313
  89.4 4.8 fusion.317
  95.3 21.9 %dynamic_update_slice.235 = f32[2,1,256,16,64]{2,0,4,3,1:T(2,128)} dynamic-update-slice(f32[2,1,256,16,64]{2,0,4,3,1:T(2,128)} %get-tuple-element.2732, f32[1,1,256,16,64]{2,0,4,3,1:T(1,128)S(1)} %copy.413, s32[]{:T(128)} %get-tuple-element.2730, s32[]{:T(128)} %constant.258.clone.1..sunk.3, s32[]{:T(128)} %constant.258.clone.1..sunk.3, s32[]{:T(128)} %constant.258.clone.1..sunk.3, ...) | dynamic-update-slice | bytes 2097156 | tf_op jit(solution)/shard_map/vmap()/while/body/jit(dynamic_update_index_in_dim)/dynamic_update_slice | solution.py:69
  117.6 3.2 fusion.313
  124.2 9.4 %all_gather.29 = f32[4,1,16]{2,1,0:T(1,128)S(1)} all-gather(f32[1,1,16]{2,1,0:T(1,128)S(1)} %exp.133), channel_id=1, replica_groups=mesh['batch'=4,'seq'=4,'head'=2] {'seq'}, dimensions={0}, use_global_device_ids=true | all-gather | bytes 320 | tf_op jit(solution)/shard_map/all_gather | solution.py:24
  138.0 3.9 transpose.187
  141.9 24.1 %all-gather.12.cloned.1.call-done = f32[4,16,64,128]{3,2,1,0:T(8,128)} async-done(((f32[1,16,64,128]{3,2,1,0:T(8,128)}), f32[4,16,64,128]{3,2,1,0:T(8,128)}) %all-gather.12.cloned.1.call-update) | async-done | bytes 2097168 | tf_op jit(solution)/shard_map/all_gather | solution.py:24
  166.0 4.8 while.118
  173.7 3.8 multiply_add_fusion
  180.4 5.5 multiply_reduce_fusion.6
  188.5 5.9 multiply_reduce_fusion
  196.8 6.6 fusion.168
  209.3 4.2 fusion.201
  220.1 46.4 %while.117 = (s32[]{:T(128)}, f32[1,16,64,128]{3,2,1,0:T(8,128)S(1)}, f32[2,1,256,256,16]{3,4,2,1,0:T(8,128)}, f32[2,1,128,256]{2,3,1,0:T(8,128)}, f32[2,1,256,1...) while((s32[]{:T(128)}, ...), condition=%wide.region_19.20_spmd.clone.clone, body=%wide.region_16.19_spmd.clone.clone.sunk | while | flops 912007232 | bytes 91645848 | solution.py:69
  225.2 6.3 multiply_dynamic-update-slice_fusion.4
  248.4 6.3 multiply_dynamic-update-slice_fusion.4
  266.5 4.5 reshape.1300
  271.0 4.5 copy.251
  275.5 7.3 while.119
  286.5 108.7 %while.121 = (s32[]{:T(128)}, f32[16]{0:T(128)}, f32[1,16,64,128]{3,2,1,0:T(8,128)S(1)}, f32[2,1,256,16,64]{2,4,3,1,0:T(8,128)}, f32[2,1,256,128]{3,2,1,0:T(8,12...) while((s32[]{:T(128)}, f32[16]{0:T(128)}, ...), condition=%wide.region_32.33_spmd.clone.clone, body=%wide.region_20.32_spmd.clone.clone.sunk | while | flops 3434913792 | bytes 128363696 | solution.py:69
  286.7 6.7 constant_dynamic-slice_fusion.20
  295.7 11.3 %fusion.331 = (f32[256,16]{0,1:T(8,128)}, f32[256,16]{0,1:T(8,128)}, f32[256,256]{1,0:T(8,128)S(1)}) fusion(f32[1,1,256,256,16]{3,4,2,1,0:T(8,128)S(1)} %constant_dynamic-slice_fusion.23, f32[256,256]{1,0:T(8,128)S(1)} %dynamic-slice_bitcast_fusion.8, pred[256,256]{1,0:T(8,128)(4,1)S(1)} %get-tuple-element.2976, ...), kind=kOutput, calls=%fused_computation.161.clone.1 | convolution fusion | flops 813621248 | bytes 11109376 | tf_op jit(solution)/shard_map/transpose(jvp(vmap()))/while/body/eval_jaxpr/tsh,shp->thp/dot_general | solution.py:61
  317.5 8.9 %fusion.330 = (f32[256,16]{0,1:T(8,128)S(1)}, f32[1,256,16,64]{1,3,2,0:T(8,128)}) fusion(f32[2,1,256,16,64]{2,4,3,1,0:T(8,128)} %get-tuple-element.2974, s32[]{:T(128)S(6)} %sub.235, f32[1,1,256,256,16]{3,4,2,1,0:T(8,128)} %get-tuple-element.2704, f32[2,1,256,16,64]{2,4,3,1,0:T(8,128)} %get-tuple-element.2960, ...), kind=kOutput, calls=%fused_computation.139.clone.1 | convolution fusion | flops 806350848 | bytes 8422400 | tf_op jit(solution)/shard_map/transpose(jvp(vmap()))/while/body/eval_jaxpr/tsh,shp->thp/dot_general | solution.py:61
  330.8 3.3 convolution_bitcast_fusion.11
  340.8 6.7 constant_dynamic-slice_fusion.20
  349.9 11.3 %fusion.331 = (f32[256,16]{0,1:T(8,128)}, f32[256,16]{0,1:T(8,128)}, f32[256,256]{1,0:T(8,128)S(1)}) fusion(f32[1,1,256,256,16]{3,4,2,1,0:T(8,128)S(1)} %constant_dynamic-slice_fusion.23, f32[256,256]{1,0:T(8,128)S(1)} %dynamic-slice_bitcast_fusion.8, pred[256,256]{1,0:T(8,128)(4,1)S(1)} %get-tuple-element.2976, ...), kind=kOutput, calls=%fused_computation.161.clone.1 | convolution fusion | flops 813621248 | bytes 11109376 | tf_op jit(solution)/shard_map/transpose(jvp(vmap()))/while/body/eval_jaxpr/tsh,shp->thp/dot_general | solution.py:61
  371.6 8.9 %fusion.330 = (f32[256,16]{0,1:T(8,128)S(1)}, f32[1,256,16,64]{1,3,2,0:T(8,128)}) fusion(f32[2,1,256,16,64]{2,4,3,1,0:T(8,128)} %get-tuple-element.2974, s32[]{:T(128)S(6)} %sub.235, f32[1,1,256,256,16]{3,4,2,1,0:T(8,128)} %get-tuple-element.2704, f32[2,1,256,16,64]{2,4,3,1,0:T(8,128)} %get-tuple-element.2960, ...), kind=kOutput, calls=%fused_computation.139.clone.1 | convolution fusion | flops 806350848 | bytes 8422400 | tf_op jit(solution)/shard_map/transpose(jvp(vmap()))/while/body/eval_jaxpr/tsh,shp->thp/dot_general | solution.py:61
  384.9 3.3 convolution_bitcast_fusion.11
  395.2 4.9 fusion.214
  404.0 4.9 copy.266
  408.8 4.9 reshape.1301
  413.8 6.4 fusion.222
  422.2 3.7 collective-permute-done.2
  431.7 4.8 fusion.218
  436.6 3.4 fusion.177
  445.1 3.4 fusion.174
  455.9 3.7 multiply_reduce_fusion.7
  462.0 81.9 %all-reduce.2 = (f32[512]{0:T(512)}, f32[4,1024]{1,0:T(4,128)}, f32[1024]{0:T(1024)}, f32[4,256]{1,0:T(4,128)}, f32[256]{0:T(256)}, /*index=5*/f32[16]{0:T(128)}, f32[16]{0:T(128)}, f32[16]{0:T(128)}, f32[1024]{0:T(1024)}) all-reduce(f32[512]{0:T(512)S(1)} %get-tuple-element.1965, ...), channel_id=1, replica_groups=mesh['batch'=4,'seq'=4,'head'=2] {'batch','seq'}, use_global_device_ids=true, to_apply=%region_39.40 | all-reduce | flops 7984 | bytes 63872 | tf_op jit(solution)/shard_map/psum | solution.py:261
  546.9 290.1 %all-reduce.8.cloned.1.call-done = (f32[1024,1024]{1,0:T(8,128)}, f32[1024,1024]{1,0:T(8,128)}, f32[1024,16]{0,1:T(8,128)}, f32[1024,256]{1,0:T(8,128)}, f32[1024,1024]{1,0:T(8,128)}) async-done(((f32[1024,1024]{1,0:T(8,128)}, f32[1024,1024]{1,0:T(8,128)}, f32[1024,16]{0,1:T(8,128)}, f32[1024,256]{1,0:T(8,128)}, f32[1024,1024]{1,0:T(8,128)}), (f32[1024,1024]{1,0:T(8,128)}, f32[1024,1024]{1,0:T(8,128)}, ...) | async-done | bytes 13697040 | tf_op jit(solution)/shard_map/psum | solution.py:261
  837.0 4.9 copy.557
  (595 shorter events, 195.1 us)
Async XLA Ops:
  7.2 173.2 %copy-start = (bf16[1024,1024]{1,0:T(8,128)(2,1)S(1)}, bf16[1024,1024]{1,0:T(8,128)(2,1)}, u32[]{:S(2)}) copy-start(bf16[1024,1024]{1,0:T(8,128)(2,1)} %param.28) | copy-start | bytes 6291460
  7.2 14.1 %all-gather.8.cloned.1.call-start = ((), (), s32[]{:S(2)}) async-start(), calls=%async_computation.2 | async-start | bytes 1572864 | tf_op jit(solution)/shard_map/all_gather | solution.py:132
  7.9 158.0 %all-gather.12.cloned.1.call-start = ((), (), s32[]{:S(2)}) async-start(), calls=%async_computation.6 | async-start | bytes 2621440 | tf_op jit(solution)/shard_map/all_gather | solution.py:24
  10.7 169.8 %copy-start.55 = (f32[2,1,512]{2,1,0:T(1,128)}, f32[2,1,512]{2,1,0:T(1,128)S(1)}, u32[]{:S(2)}) copy-start(f32[2,1,512]{2,1,0:T(1,128)S(1)} %convert_element_type.86) | copy-start | bytes 12292
  12.7 23.3 %copy-start.85 = (f32[1,256]{1,0:T(1,128)}, f32[1,256]{1,0:T(1,128)S(1)}, u32[]{:S(2)}) copy-start(f32[1,256]{1,0:T(1,128)S(1)} %get-tuple-element.2197) | copy-start | bytes 3076
  12.7 23.3 %copy-start.87 = (f32[1,256]{1,0:T(1,128)}, f32[1,256]{1,0:T(1,128)S(1)}, u32[]{:S(2)}) copy-start(f32[1,256]{1,0:T(1,128)S(1)} %get-tuple-element.2198) | copy-start | bytes 3076
  12.7 23.3 %copy-start.89 = (f32[1,256]{1,0:T(1,128)}, f32[1,256]{1,0:T(1,128)S(1)}, u32[]{:S(2)}) copy-start(f32[1,256]{1,0:T(1,128)S(1)} %get-tuple-element.2199) | copy-start | bytes 3076
  12.7 23.3 %copy-start.91 = (f32[1,256]{1,0:T(1,128)}, f32[1,256]{1,0:T(1,128)S(1)}, u32[]{:S(2)}) copy-start(f32[1,256]{1,0:T(1,128)S(1)} %get-tuple-element.2200) | copy-start | bytes 3076
  13.6 23.6 %copy-start.68 = (f32[1,1024]{1,0:T(1,128)}, f32[1,1024]{1,0:T(1,128)S(1)}, u32[]{:S(2)}) copy-start(f32[1,1024]{1,0:T(1,128)S(1)} %get-tuple-element.2193) | copy-start | bytes 12292
  13.6 23.6 %copy-start.70 = (f32[1,1024]{1,0:T(1,128)}, f32[1,1024]{1,0:T(1,128)S(1)}, u32[]{:S(2)}) copy-start(f32[1,1024]{1,0:T(1,128)S(1)} %get-tuple-element.2194) | copy-start | bytes 12292
  13.6 23.6 %copy-start.72 = (f32[1,1024]{1,0:T(1,128)}, f32[1,1024]{1,0:T(1,128)S(1)}, u32[]{:S(2)}) copy-start(f32[1,1024]{1,0:T(1,128)S(1)} %get-tuple-element.2195) | copy-start | bytes 12292
  13.6 23.6 %copy-start.74 = (f32[1,1024]{1,0:T(1,128)}, f32[1,1024]{1,0:T(1,128)S(1)}, u32[]{:S(2)}) copy-start(f32[1,1024]{1,0:T(1,128)S(1)} %get-tuple-element.2196) | copy-start | bytes 12292
  21.3 7.4 copy-start.24
  21.3 7.4 copy-start.41
  23.0 157.4 %copy-start.63 = (f32[512]{0:T(512)}, f32[512]{0:T(512)S(1)}, u32[]{:S(2)}) copy-start(f32[512]{0:T(512)S(1)} %add_rsqrt_fusion.1) | copy-start | bytes 6148
  24.9 11.1 %copy-start.30 = (f32[512,256]{1,0:T(8,128)}, f32[512,256]{1,0:T(8,128)S(1)}, u32[]{:S(2)}) copy-start(f32[512,256]{1,0:T(8,128)S(1)} %fusion.220) | copy-start | bytes 1572868
  24.9 9.9 %copy-start.76 = (bf16[1024,16]{0,1:T(8,128)(2,1)S(1)}, bf16[1024,16]{0,1:T(8,128)(2,1)}, u32[]{:S(2)}) copy-start(bf16[1024,16]{0,1:T(8,128)(2,1)} %param.30) | copy-start | bytes 98308
  24.9 9.9 %copy-start.100 = (f32[16]{0:T(128)S(1)}, f32[16]{0:T(128)}, u32[]{:S(2)}) copy-start(f32[16]{0:T(128)} %param.36) | copy-start | bytes 196
  24.9 11.0 %collective-permute-start.1 = (f32[1,3,256]{2,1,0:T(4,128)S(1)}, f32[1,3,256]{2,1,0:T(4,128)S(1)}, u32[]{:S(2)}, u32[]{:S(2)}) collective-permute-start(f32[1,3,256]{2,1,0:T(4,128)S(1)} %slice.201), channel_id=1, source_target_pairs={{0,2},{2,4},{4,6},{1,3},{3,5},{5,7},{8,10},{10,12},{12,14},{9,11},... | collective-permute-start | bytes 9224 | tf_op jit(solution)/shard_map/ppermute | solution.py:19
  31.4 5.8 collective-permute-start
  120.8 67.6 %all-gather.10.cloned.1.call-start = ((), (), s32[]{:S(2)}) async-start(), calls=%async_computation.4 | async-start | bytes 1572864 | tf_op jit(solution)/shard_map/all_gather | solution.py:133
  121.6 154.0 %all-gather.14.cloned.1.call-start = ((), (), s32[]{:S(2)}) async-start(), calls=%async_computation.7 | async-start | bytes 2621440 | tf_op jit(solution)/shard_map/all_gather | solution.py:24
  180.4 8.0 copy-start.61
  188.4 8.4 copy-start.78
  196.8 7.9 copy-start.31
  213.6 227.5 %all-reduce.10.cloned.1.call-start = ((), (), s32[]{:S(2)}) async-start(), calls=%async_computation.9 | async-start | bytes 1048576 | tf_op jit(solution)/shard_map/psum | solution.py:213
  225.2 7.3 copy-start.21
  235.8 7.4 copy-start.50
  236.0 7.3 copy-start.53
  248.4 7.3 copy-start.21
  259.0 7.4 copy-start.50
  259.2 7.3 copy-start.53
  317.5 13.2 %copy-start.57 = (f32[2,1,256,16,1]{2,0,4,3,1:T(2,128)S(1)}, f32[2,1,256,16,1]{2,0,4,3,1:T(2,128)}, u32[]{:S(2)}) copy-start(f32[2,1,256,16,1]{2,0,4,3,1:T(2,128)} %get-tuple-element.2966) | copy-start | bytes 98308 | tf_op jit(solution)/shard_map/transpose(jvp(vmap()))/while
  329.3 7.3 copy-start.47
  330.8 7.7 copy-start.5
  371.6 13.2 %copy-start.57 = (f32[2,1,256,16,1]{2,0,4,3,1:T(2,128)S(1)}, f32[2,1,256,16,1]{2,0,4,3,1:T(2,128)}, u32[]{:S(2)}) copy-start(f32[2,1,256,16,1]{2,0,4,3,1:T(2,128)} %get-tuple-element.2966) | copy-start | bytes 98308 | tf_op jit(solution)/shard_map/transpose(jvp(vmap()))/while
  383.5 7.3 copy-start.23
  383.5 7.3 copy-start.47
  384.9 7.7 copy-start.5
  395.2 58.2 %reduce-scatter.3.cloned.1.call-start = ((), (), s32[]{:S(2)}) async-start(), calls=%async_computation.3 | async-start | bytes 3145728 | tf_op jit(solution)/shard_map/reduce_scatter | solution.py:187
  400.2 55.8 %reduce-scatter.5.cloned.1.call-start = ((), (), s32[]{:S(2)}) async-start(), calls=%async_computation.5 | async-start | bytes 3145728 | tf_op jit(solution)/shard_map/reduce_scatter | solution.py:249
  413.7 7.8 copy-start.60
  413.8 7.8 copy-start.59
  413.8 8.0 copy-start.77
  420.3 5.6 collective-permute-start.2
  430.5 406.5 %all-reduce.8.cloned.1.call-start = ((), (), s32[]{:S(2)}) async-start(), calls=%async_computation.8 | async-start | bytes 27394048 | tf_op jit(solution)/shard_map/psum | solution.py:261
  443.6 5.5 collective-permute-start.3
  455.9 88.0 %copy-start.35 = (f32[512,512]{1,0:T(8,128)S(1)}, f32[512,512]{1,0:T(8,128)}, u32[]{:S(2)}) copy-start(f32[512,512]{1,0:T(8,128)} %reduce-scatter.5.cloned.1.call-done) | copy-start | bytes 3145732
  (108 other events, 385.6 us)
Sparse Core Ops, SparseCore 0:
  9.5 11.7 all-gather.7
  121.0 44.9 all-gather.11
  167.5 7.8 all-gather.9
  213.7 44.5 all-gather.13
  395.3 17.5 all-reduce.9
  415.0 10.8 reduce-scatter.2
  430.6 8.5 reduce-scatter.4
  451.1 385.9 all-reduce.7
where the time goes:
time: 872 us; the launch traced here: 856 us
  waiting for transfers between devices  328 us (38%)
  local copies, waits for them, and re-layouts  169 us (19%)
  matrix products  141 us (16%)
  blocking collectives  101 us (12%)
  other arithmetic  90.1 us (10%)
  between operations  15.5 us (2%)
  starting transfers between devices  10.8 us (1%)
    psum x1, waiting for transfers between devices, on_device(): lax.psum((grad_norm_gain, grad_gate_weight, grad_inner_weight, grad_step_...  290 us
    psum x1, blocking collectives, on_device(): lax.psum((grad_norm_gain, grad_gate_weight, grad_inner_weight, grad_step_...  81.9 us
    dynamic_update_slice x24, local copies, waits for them, and re-layouts, ssd_blocks(): lax.scan(advance, initial, (inner_blocks, write_blocks, read_blocks, step...  63.8 us
    dot_general x6, matrix products, advance(): jnp.einsum('tsh,shp->thp', decays * scores[:, :, None], weighted, precisi...  50 us
    unnamed x150, local copies, waits for them, and re-layouts  26.9 us
    all_gather x2, waiting for transfers between devices, entering(): everything = jax.tree.map(lambda part: lax.all_gather(part, axis), array)  24.1 us
    dynamic_slice x18, local copies, waits for them, and re-layouts, ssd_blocks(): lax.scan(advance, initial, (inner_blocks, write_blocks, read_blocks, step...  17.4 us
  transfers between devices with their start and end apart: 12, of which 5 were waited for; matrix products, arithmetic and copies ran while one was open for 18% of the time, Pallas kernels for 0%

commit v1 on v0

--- a/solution.py
+++ b/solution.py
@@ -259,23 +259,26 @@
     grad_hidden = grad_rows.reshape(seq_count, tok_count, local_width)
     grad_norm_gain = jnp.sum(input_share * normal_local, axis=0)
     summed = lax.psum(
-        (
-            grad_norm_gain,
-            grad_gate_weight,
-            grad_inner_weight,
-            grad_step_weight,
-            grad_maps_weight,
-            grad_inner_kernel,
-            grad_inner_bias,
-            grad_maps_kernel,
-            grad_maps_bias,
-            grad_step_bias,
-            grad_decay_log,
-            grad_skip_gain,
-            grad_gate_gain,
-            grad_output_weight,
+        lax.psum(
+            (
+                grad_norm_gain,
+                grad_gate_weight,
+                grad_inner_weight,
+                grad_step_weight,
+                grad_maps_weight,
+                grad_inner_kernel,
+                grad_inner_bias,
+                grad_maps_kernel,
+                grad_maps_bias,
+                grad_step_bias,
+                grad_decay_log,
+                grad_skip_gain,
+                grad_gate_gain,
+                grad_output_weight,
+            ),
+            axis_name="seq",
         ),
-        ("batch", "seq"),
+        axis_name="batch",
     )
     return (
         output,

time: 872 us -> 1240 us (1.42)
  waiting for transfers between devices: 328 us -> 734 us
  blocking collectives: 101 us -> 57.6 us
    psum x0 -> x1, waiting for transfers between devices: none -> 218 us  [on_device(): lax.psum(lax.psum((grad_norm_gain, grad_gate_weight, grad_inner_weight, g...]
    psum x1, waiting for transfers between devices: 290 us -> 451 us  [on_device(): lax.psum((grad_norm_gain, grad_gate_weight, grad_inner_weight, grad_step_...]
    psum x1, blocking collectives: 81.9 us -> 19.7 us  [on_device(): lax.psum((grad_norm_gain, grad_gate_weight, grad_inner_weight, grad_step_...]
    psum x0 -> x1, blocking collectives: none -> 19.3 us  [on_device(): lax.psum(lax.psum((grad_norm_gain, grad_gate_weight, grad_inner_weight, g...]
    unnamed x150 -> x152, local copies, waits for them, and re-layouts: 26.9 us -> 26.6 us
  transfers between devices with their start and end apart: 12 -> 13, of which waited for: 5 -> 9; matrix products, arithmetic and copies ran while one was open for 18% -> 11% of each run, Pallas kernels for 0% -> 0%
where the time goes in v1:
time: 1240 us; the launch traced here: 1220 us
  waiting for transfers between devices  734 us (59%)
  local copies, waits for them, and re-layouts  171 us (14%)
  matrix products  140 us (11%)
  other arithmetic  91.6 us (7%)
  blocking collectives  57.6 us (5%)
  between operations  15.2 us (1%)
    psum x1, waiting for transfers between devices, on_device(): lax.psum((grad_norm_gain, grad_gate_weight, grad_inner_weight, grad_step_...  451 us
    psum x1, waiting for transfers between devices, on_device(): lax.psum(lax.psum((grad_norm_gain, grad_gate_weight, grad_inner_weight, g...  218 us
    dynamic_update_slice x24, local copies, waits for them, and re-layouts, ssd_blocks(): lax.scan(advance, initial, (inner_blocks, write_blocks, read_blocks, step...  63.8 us
    dot_general x6, matrix products, advance(): jnp.einsum('tsh,shp->thp', decays * scores[:, :, None], weighted, precisi...  50 us
    unnamed x152, local copies, waits for them, and re-layouts  26.6 us
  transfers between devices with their start and end apart: 13, of which 9 were waited for; matrix products, arithmetic and copies ran while one was open for 11% of the time, Pallas kernels for 0%

profile of v1, /device:TPU:0, one launch (start us, length us, event | category | flops | bytes accessed | tf_op | source)
XLA Modules:
  0.0 1222.3 jit_solution(14390496715083658674)
XLA Ops:
  13.6 7.7 all-gather.8.cloned.1.call-done
  24.9 3.8 collective-permute-start.1
  31.4 3.4 collective-permute-start
  43.3 3.5 reshape_reshape.7
  50.0 70.7 %while.120 = (s32[]{:T(128)}, f32[1,16,64,128]{3,2,1,0:T(8,128)}, f32[2,1,256,16,64]{2,0,4,3,1:T(2,128)}, f32[2,1,256,16]{2,0,3,1:T(2,128)}, f32[16]{0:T(128)S(1...) while((s32[]{:T(128)}, f32[1,16,64,128]{3,2,1,0:T(8,128)}, ...), condition=%wide.region_4.5_spmd.clone.clone, body=%wide.region_1.4_spmd.clone.clone.sunk | while | flops 1717903360 | bytes 23170916 | solution.py:69
  53.5 4.8 fusion.317
  59.4 21.9 %dynamic_update_slice.235 = f32[2,1,256,16,64]{2,0,4,3,1:T(2,128)} dynamic-update-slice(f32[2,1,256,16,64]{2,0,4,3,1:T(2,128)} %get-tuple-element.2746, f32[1,1,256,16,64]{2,0,4,3,1:T(1,128)S(1)} %copy.413, s32[]{:T(128)} %get-tuple-element.2744, s32[]{:T(128)} %constant.258.clone.1..sunk.3, s32[]{:T(128)} %constant.258.clone.1..sunk.3, s32[]{:T(128)} %constant.258.clone.1..sunk.3, ...) | dynamic-update-slice | bytes 2097156 | tf_op jit(solution)/shard_map/vmap()/while/body/jit(dynamic_update_index_in_dim)/dynamic_update_slice | solution.py:69
  89.3 4.8 fusion.317
  95.2 21.9 %dynamic_update_slice.235 = f32[2,1,256,16,64]{2,0,4,3,1:T(2,128)} dynamic-update-slice(f32[2,1,256,16,64]{2,0,4,3,1:T(2,128)} %get-tuple-element.2746, f32[1,1,256,16,64]{2,0,4,3,1:T(1,128)S(1)} %copy.413, s32[]{:T(128)} %get-tuple-element.2744, s32[]{:T(128)} %constant.258.clone.1..sunk.3, s32[]{:T(128)} %constant.258.clone.1..sunk.3, s32[]{:T(128)} %constant.258.clone.1..sunk.3, ...) | dynamic-update-slice | bytes 2097156 | tf_op jit(solution)/shard_map/vmap()/while/body/jit(dynamic_update_index_in_dim)/dynamic_update_slice | solution.py:69
  124.8 9.3 all_gather.29
  138.7 3.9 transpose.187
  142.6 23.3 %all-gather.12.cloned.1.call-done = f32[4,16,64,128]{3,2,1,0:T(8,128)} async-done(((f32[1,16,64,128]{3,2,1,0:T(8,128)}), f32[4,16,64,128]{3,2,1,0:T(8,128)}) %all-gather.12.cloned.1.call-update) | async-done | bytes 2097168 | tf_op jit(solution)/shard_map/all_gather | solution.py:24
  165.9 4.8 while.118
  173.7 3.8 multiply_add_fusion
  180.4 5.5 multiply_reduce_fusion.6
  188.4 5.9 multiply_reduce_fusion
  196.7 6.6 fusion.168
  209.2 4.2 fusion.201
  220.0 46.4 %while.117 = (s32[]{:T(128)}, f32[1,16,64,128]{3,2,1,0:T(8,128)S(1)}, f32[2,1,256,256,16]{3,4,2,1,0:T(8,128)}, f32[2,1,128,256]{2,3,1,0:T(8,128)}, f32[2,1,256,1...) while((s32[]{:T(128)}, ...), condition=%wide.region_19.20_spmd.clone.clone, body=%wide.region_16.19_spmd.clone.clone.sunk | while | flops 912007232 | bytes 91645848 | solution.py:69
  225.1 6.2 multiply_dynamic-update-slice_fusion.4
  248.3 6.3 multiply_dynamic-update-slice_fusion.4
  266.4 4.5 reshape.1300
  270.9 4.5 copy.251
  275.5 5.1 fusion.218
  280.6 3.4 fusion.177
  284.0 7.4 while.119
  295.2 106.7 %while.121 = (s32[]{:T(128)}, f32[16]{0:T(128)}, f32[1,16,64,128]{3,2,1,0:T(8,128)S(1)}, f32[2,1,256,16,64]{2,4,3,1,0:T(8,128)}, f32[2,1,256,128]{3,2,1,0:T(8,12...) while((s32[]{:T(128)}, f32[16]{0:T(128)}, ...), condition=%wide.region_32.33_spmd.clone.clone, body=%wide.region_20.32_spmd.clone.clone.sunk | while | flops 3434913792 | bytes 128233152 | solution.py:69
  295.3 6.7 constant_dynamic-slice_fusion.20
  304.4 11.3 fusion.331
  326.2 8.9 fusion.330
  348.5 6.7 constant_dynamic-slice_fusion.20
  357.6 11.3 fusion.331
  379.4 8.9 fusion.330
  391.6 3.3 convolution_bitcast_fusion.11
  401.9 4.9 copy.266
  406.7 4.9 reshape.1301
  411.6 6.8 fusion.222
  425.4 5.7 fusion.162
  431.2 9.9 all-reduce.15.cloned.1.call-done
  445.1 3.4 fusion.174
  451.8 4.9 fusion.214
  463.6 451.4 %all-reduce.11.cloned.1.call-done = (f32[1024,1024]{1,0:T(8,128)}, f32[1024,1024]{1,0:T(8,128)}, f32[1024,16]{0,1:T(8,128)}, f32[1024,256]{1,0:T(8,128)}, f32[1024,1024]{1,0:T(8,128)}) async-done(((f32[1024,1024]{1,0:T(8,128)}, f32[1024,1024]{1,0:T(8,128)}, f32[1024,16]{0,1:T(8,128)}, f32[1024,256]{1,0:T(8,128)}, f32[1024,1024]{1,0:T(8,128)}), (f32[1024,1024]{1,0:T(8,128)}, f32[1024,1024]{1,0:T(8,128)}, ...) | async-done | bytes 13697040 | tf_op jit(solution)/shard_map/psum | solution.py:262
  917.5 8.3 reduce-scatter.3.cloned.1.call-done
  928.3 10.7 reduce-scatter.5.cloned.1.call-done
  942.0 19.7 %all-reduce.2 = (f32[512]{0:T(512)S(1)}, f32[4,1024]{1,0:T(4,128)S(1)}, f32[1024]{0:T(1024)S(1)}, f32[4,256]{1,0:T(4,128)S(1)}, f32[256]{0:T(256)S(1)}, /*index=...) all-reduce(f32[512]{0:T(512)S(1)} %get-tuple-element.1965, ...), channel_id=1, replica_groups=mesh['batch'=4,'seq'=4,'head'=2] {'seq'}, use_global_device_ids=true, to_apply=%region_39.40 | all-reduce | flops 7984 | bytes 63872 | tf_op jit(solution)/shard_map/psum | solution.py:262
  961.7 19.3 %all-reduce.4 = (f32[512]{0:T(512)}, f32[4,1024]{1,0:T(4,128)}, f32[1024]{0:T(1024)}, f32[4,256]{1,0:T(4,128)}, f32[256]{0:T(256)}, /*index=5*/f32[16]{0:T(128)}, f32[16]{0:T(128)}, f32[16]{0:T(128)}, f32[1024]{0:T(1024)}) all-reduce(f32[512]{0:T(512)S(1)} %get-tuple-element.2124, ...), channel_id=1, replica_groups=mesh['batch'=4,'seq'=4,'head'=2] {'batch'}, use_global_device_ids=true, to_apply=%region_40.41 | all-reduce | flops 7984 | bytes 63872 | tf_op jit(solution)/shard_map/psum | solution.py:261
  986.5 217.5 %all-reduce.13.cloned.1.call-done = (f32[1024,1024]{1,0:T(8,128)}, f32[1024,1024]{1,0:T(8,128)}, f32[1024,16]{0,1:T(8,128)}, f32[1024,256]{1,0:T(8,128)}, f32[1024,1024]{1,0:T(8,128)}) async-done(((f32[1024,1024]{1,0:T(8,128)}, f32[1024,1024]{1,0:T(8,128)}, f32[1024,16]{0,1:T(8,128)}, f32[1024,256]{1,0:T(8,128)}, f32[1024,1024]{1,0:T(8,128)}), (f32[1024,1024]{1,0:T(8,128)}, f32[1024,1024]{1,0:T(8,128)}, ...) | async-done | bytes 13697040 | tf_op jit(solution)/shard_map/psum | solution.py:261
  1204.0 4.9 copy.562
  (605 shorter events, 211.6 us)
Async XLA Ops:
  7.2 173.2 %copy-start = (bf16[1024,1024]{1,0:T(8,128)(2,1)S(1)}, bf16[1024,1024]{1,0:T(8,128)(2,1)}, u32[]{:S(2)}) copy-start(bf16[1024,1024]{1,0:T(8,128)(2,1)} %param.28) | copy-start | bytes 6291460
  7.2 14.1 %all-gather.8.cloned.1.call-start = ((), (), s32[]{:S(2)}) async-start(), calls=%async_computation.2 | async-start | bytes 1572864 | tf_op jit(solution)/shard_map/all_gather | solution.py:132
  7.9 158.0 %all-gather.12.cloned.1.call-start = ((), (), s32[]{:S(2)}) async-start(), calls=%async_computation.6 | async-start | bytes 2621440 | tf_op jit(solution)/shard_map/all_gather | solution.py:24
  10.7 169.7 %copy-start.54 = (f32[2,1,512]{2,1,0:T(1,128)}, f32[2,1,512]{2,1,0:T(1,128)S(1)}, u32[]{:S(2)}) copy-start(f32[2,1,512]{2,1,0:T(1,128)S(1)} %convert_element_type.86) | copy-start | bytes 12292
  12.7 23.3 %copy-start.88 = (f32[1,256]{1,0:T(1,128)}, f32[1,256]{1,0:T(1,128)S(1)}, u32[]{:S(2)}) copy-start(f32[1,256]{1,0:T(1,128)S(1)} %get-tuple-element.2211) | copy-start | bytes 3076
  12.7 23.3 %copy-start.90 = (f32[1,256]{1,0:T(1,128)}, f32[1,256]{1,0:T(1,128)S(1)}, u32[]{:S(2)}) copy-start(f32[1,256]{1,0:T(1,128)S(1)} %get-tuple-element.2212) | copy-start | bytes 3076
  12.7 23.3 %copy-start.92 = (f32[1,256]{1,0:T(1,128)}, f32[1,256]{1,0:T(1,128)S(1)}, u32[]{:S(2)}) copy-start(f32[1,256]{1,0:T(1,128)S(1)} %get-tuple-element.2213) | copy-start | bytes 3076
  12.7 23.3 %copy-start.94 = (f32[1,256]{1,0:T(1,128)}, f32[1,256]{1,0:T(1,128)S(1)}, u32[]{:S(2)}) copy-start(f32[1,256]{1,0:T(1,128)S(1)} %get-tuple-element.2214) | copy-start | bytes 3076
  13.6 23.7 %copy-start.67 = (f32[1,1024]{1,0:T(1,128)}, f32[1,1024]{1,0:T(1,128)S(1)}, u32[]{:S(2)}) copy-start(f32[1,1024]{1,0:T(1,128)S(1)} %get-tuple-element.2207) | copy-start | bytes 12292
  13.6 23.7 %copy-start.69 = (f32[1,1024]{1,0:T(1,128)}, f32[1,1024]{1,0:T(1,128)S(1)}, u32[]{:S(2)}) copy-start(f32[1,1024]{1,0:T(1,128)S(1)} %get-tuple-element.2208) | copy-start | bytes 12292
  13.6 23.7 %copy-start.71 = (f32[1,1024]{1,0:T(1,128)}, f32[1,1024]{1,0:T(1,128)S(1)}, u32[]{:S(2)}) copy-start(f32[1,1024]{1,0:T(1,128)S(1)} %get-tuple-element.2209) | copy-start | bytes 12292
  13.6 23.7 %copy-start.73 = (f32[1,1024]{1,0:T(1,128)}, f32[1,1024]{1,0:T(1,128)S(1)}, u32[]{:S(2)}) copy-start(f32[1,1024]{1,0:T(1,128)S(1)} %get-tuple-element.2210) | copy-start | bytes 12292
  21.3 7.4 copy-start.24
  21.3 7.4 copy-start.41
  23.0 157.4 %copy-start.61 = (f32[512]{0:T(512)}, f32[512]{0:T(512)S(1)}, u32[]{:S(2)}) copy-start(f32[512]{0:T(512)S(1)} %add_rsqrt_fusion.1) | copy-start | bytes 6148
  24.9 11.2 copy-start.31
  24.9 9.9 copy-start.75
  24.9 9.9 copy-start.102
  24.9 11.1 collective-permute-start.1
  31.4 5.8 collective-permute-start
  50.0 72.3 %copy-start.99 = (f32[16]{0:T(128)S(1)}, f32[16]{0:T(128)}, u32[]{:S(2)}) copy-start(f32[16]{0:T(128)} %param.38) | copy-start | bytes 196
  120.8 67.6 %all-gather.10.cloned.1.call-start = ((), (), s32[]{:S(2)}) async-start(), calls=%async_computation.4 | async-start | bytes 1572864 | tf_op jit(solution)/shard_map/all_gather | solution.py:133
  121.5 162.5 %all-gather.14.cloned.1.call-start = ((), (), s32[]{:S(2)}) async-start(), calls=%async_computation.7 | async-start | bytes 2621440 | tf_op jit(solution)/shard_map/all_gather | solution.py:24
  180.4 8.0 copy-start.59
  188.3 8.4 copy-start.77
  196.7 7.9 copy-start.32
  213.4 227.6 %all-reduce.15.cloned.1.call-start = ((), (), s32[]{:S(2)}) async-start(), calls=%async_computation.10 | async-start | bytes 1048576 | tf_op jit(solution)/shard_map/psum | solution.py:213
  235.7 7.4 copy-start.49
  259.0 7.4 copy-start.49
  326.2 11.3 copy-start.85
  337.5 8.6 copy-start.86
  338.5 7.7 copy-start.5
  379.4 11.3 copy-start.85
  390.7 8.6 copy-start.86
  391.6 7.7 copy-start.5
  411.6 9.5 copy-start.58
  411.6 9.5 copy-start.57
  411.6 9.7 copy-start.25
  411.6 9.7 copy-start.63
  419.8 5.6 collective-permute-start.2
  421.3 493.7 %all-reduce.11.cloned.1.call-start = ((), (), s32[]{:S(2)}) async-start(), calls=%async_computation.8 | async-start | bytes 27394048 | tf_op jit(solution)/shard_map/psum | solution.py:262
  421.3 19.8 %copy-start.81 = (f32[1,3,256]{2,1,0:T(4,128)S(1)}, f32[1,3,256]{2,1,0:T(4,128)}, u32[]{:S(2)}) copy-start(f32[1,3,256]{2,1,0:T(4,128)} %copy-done.80) | copy-start | bytes 9220
  443.8 5.5 collective-permute-start.3
  451.1 474.6 %reduce-scatter.3.cloned.1.call-start = ((), (), s32[]{:S(2)}) async-start(), calls=%async_computation.3 | async-start | bytes 3145728 | tf_op jit(solution)/shard_map/reduce_scatter | solution.py:187
  456.7 482.3 %reduce-scatter.5.cloned.1.call-start = ((), (), s32[]{:S(2)}) async-start(), calls=%async_computation.5 | async-start | bytes 3145728 | tf_op jit(solution)/shard_map/reduce_scatter | solution.py:249
  463.5 740.5 %all-reduce.13.cloned.1.call-start = ((), (), s32[]{:S(2)}) async-start(), calls=%async_computation.9 | async-start | bytes 27394048 | tf_op jit(solution)/shard_map/psum | solution.py:261
  928.3 13.7 %copy-start.98 = (f32[1024]{0:T(1024)S(1)}, f32[1024]{0:T(1024)}, u32[]{:S(2)}) copy-start(f32[1024]{0:T(1024)} %get-tuple-element.1963) | copy-start | bytes 12292
  939.0 44.5 %copy-start.36 = (f32[512,512]{1,0:T(8,128)S(1)}, f32[512,512]{1,0:T(8,128)}, u32[]{:S(2)}) copy-start(f32[512,512]{1,0:T(8,128)} %reduce-scatter.5.cloned.1.call-done) | copy-start | bytes 3145732
  (112 other events, 430.2 us)
Sparse Core Ops, SparseCore 0:
  9.5 11.7 all-gather.7
  120.9 44.9 all-gather.11
  167.5 7.8 all-gather.9
  213.6 44.5 all-gather.13
  421.4 19.6 all-reduce.14
  451.3 463.6 all-reduce.10
  917.3 8.4 reduce-scatter.2
  928.0 10.8 reduce-scatter.4
  943.3 260.6 all-reduce.12
